TPU v7x, 32 devices: a whole 2x2x4 slice. The times are simulated.
32 devices in a mesh: groups: 2 (over x), tensor: 16 (over z, y, core).
Axes of the slice: x: 2, y: 2, z: 4, core: 2. Of those that a mesh axis runs over, the one named last changes fastest.
Arguments:
- activations: bfloat16 [256, 26624], P('groups', 'tensor'), parts along dimension 0, may hold values from -6 to 6
- rotation_small: float32 [52, 52], replicated, may hold values from -0.875 to 0.875
- down_weight: bfloat16 [26624, 8192], P('tensor'), may hold values from -0.0546875 to 0.0546875
Outputs:
- projected: bfloat16 [256, 8192], P('groups', 'tensor'), parts along dimension 0
There are 2 independent parts, one for each index of `groups`. A program takes and returns all parts, laid end to end along the dimension named above; an argument that names none is the same for every part. Nothing has to cross between parts.
All inputs are finite; a program needn't handle non-finite values.
Results may differ from a plain program's by a relative error of at most 0.005.
Values sent between devices are 32-bit elements; how exact they have to be, the bound alone decides.
A program may use at most 128 MiB of HBM per device.

v0:
```python
import jax
import jax.numpy as jnp
from jax import lax
from jax.sharding import PartitionSpec as P

BLOCK = 52


def sylvester(order):
    index = jnp.arange(order, dtype=jnp.int32)
    common = jnp.zeros((order, order), jnp.int32)
    for place in range(max(order.bit_length(), 1)):
        common = common + (index[:, None] >> place & 1) * (index[None, :] >> place & 1)
    return (1 - 2 * (common % 2)).astype(jnp.float32)


def body(activations, rotation_small, down_weight):
    tokens, local = activations.shape
    shards = lax.axis_size("tensor")
    span = local // BLOCK
    kronecker = jnp.kron(sylvester(span), rotation_small)
    factor = (span * shards) ** (-0.5)
    values = activations.astype(jnp.float32)
    gathered = lax.all_to_all(values, "tensor", split_axis=0, concat_axis=1, tiled=True)
    gathered = gathered.reshape(-1, shards, local)
    gathered = jnp.einsum(
        "rsl,su->rul", gathered, sylvester(shards), precision=lax.Precision.HIGHEST
    )
    gathered = jnp.dot(gathered.reshape(-1, local), kronecker, precision=lax.Precision.HIGHEST)
    gathered = gathered.reshape(-1, shards * local)
    returned = lax.all_to_all(gathered, "tensor", split_axis=1, concat_axis=0, tiled=True)
    rotated = (returned * factor).astype(jnp.bfloat16)
    summed = lax.psum_scatter(
        lax.dot_general(
            down_weight, rotated, (((0,), (1,)), ((), ())), preferred_element_type=jnp.float32
        ),
        "tensor",
        scatter_dimension=0,
        tiled=True,
    )
    return summed.T.astype(jnp.bfloat16)


def solution(mesh):
    placed = (P("groups", "tensor"), P(), P("tensor", None))
    return jax.shard_map(
        body, mesh=mesh, in_specs=placed, out_specs=P("groups", "tensor"), check_vma=False
    )
```

profile of v0, /device:TPU:8, one launch (start us, length us, event | category | flops | bytes accessed | tf_op | source)
XLA Modules:
  0.0 187.4 jit_solution(4873965791969258324)
XLA Ops:
  6.5 2.0 %bitcast_convert_fusion = f32[16,8,1664]{2,1,0:T(8,128)} fusion(bf16[128,1664]{1,0:T(8,128)(2,1)} %param.3), kind=kLoop, calls=%fused_computation.9 | loop fusion | flops 212992 | bytes 1277952 | tf_op jit(solution)/shard_map/all_to_all | solution.py:24
  8.5 6.3 %all-to-all-start = ((f32[16,8,1664]{2,1,0:T(8,128)}), f32[16,8,1664]{2,1,0:T(8,128)S(1)}, u32[]{:S(2)}, u32[]{:S(2)}) async-start(f32[16,8,1664]{2,1,0:T(8,128)} %bitcast_convert_fusion), calls=%async_computation | async-start | bytes 1703936 | tf_op jit(solution)/shard_map/all_to_all | solution.py:24
  14.8 0.0 reduce-scatter.2.cloned.1.call-start
  14.9 0.1 fusion.10
  15.0 13.3 %broadcast_multiply_fusion = f32[32,52,32,52]{3,2,1,0:T(8,128)} fusion(f32[52,52]{1,0:T(8,128)} %param.4, f32[32,32]{1,0:T(8,128)S(1)} %fusion.10), kind=kLoop, calls=%fused_computation | loop fusion | flops 2768896 | bytes 11090496 | tf_op jit(solution)/shard_map/jit(kron)/mul | solution.py:21
  28.4 25.8 %reshape.360 = f32[1664,1664,1]{1,0,2:T(8,128)} reshape(f32[32,52,32,52]{3,2,1,0:T(8,128)} %broadcast_multiply_fusion) | data formatting | bytes 22151168 | tf_op jit(solution)/shard_map/jit(kron)/mul | solution.py:21
  54.2 0.0 all-to-all-done
  54.2 0.9 convolution_bitcast_fusion.1
  55.1 10.5 %fusion.1 = f32[8,16,1664]{2,0,1:T(8,128)S(1)} fusion(f32[1664,1664,1]{1,0,2:T(8,128)} %reshape.360, f32[8,16,1664]{2,1,0:T(8,128)S(1)} %convolution_bitcast_fusion.1), kind=kOutput, calls=%fused_computation.4 | convolution fusion | flops 4253024256 | bytes 12779520 | tf_op jit(solution)/shard_map/dot_general | solution.py:29
  65.6 26.6 %all_to_all.30 = f32[8,16,1664]{2,0,1:T(8,128)S(1)} all-to-all(f32[8,16,1664]{2,0,1:T(8,128)S(1)} %fusion.1), channel_id=1, replica_groups=mesh['groups'=2,'tensor'=16] {'tensor'}, dimensions={1} | all-to-all | bytes 1703936 | tf_op jit(solution)/shard_map/all_to_all | solution.py:31
  92.2 14.7 %convolution_bitcast_fusion = f32[8192,128]{0,1:T(8,128)} fusion(bf16[1664,8192]{1,0:T(8,128)(2,1)} %param.5, f32[8,16,1664]{2,0,1:T(8,128)S(1)} %all_to_all.30), kind=kOutput, calls=%fused_computation.1 | convolution fusion | flops 3490086912 | bytes 32309248 | tf_op jit(solution)/shard_map/dot_general | solution.py:34
  106.9 0.0 reduce-scatter.2.cloned.1.call-update
  106.9 72.0 %reduce-scatter.2.cloned.1.call-done = f32[512,128]{0,1:T(8,128)} async-done(((f32[8192,128]{0,1:T(8,128)}), f32[512,128]{0,1:T(8,128)}) %reduce-scatter.2.cloned.1.call-update) | async-done | bytes 262160 | tf_op jit(solution)/shard_map/reduce_scatter | solution.py:33
  178.9 1.6 convert_bitcast_fusion
  (6 shorter events, 0.0 us)
Async XLA Ops:
  8.5 45.7 %all-to-all-start = ((f32[16,8,1664]{2,1,0:T(8,128)}), f32[16,8,1664]{2,1,0:T(8,128)S(1)}, u32[]{:S(2)}, u32[]{:S(2)}) async-start(f32[16,8,1664]{2,1,0:T(8,128)} %bitcast_convert_fusion), calls=%async_computation | async-start | bytes 1703936 | tf_op jit(solution)/shard_map/all_to_all | solution.py:24
  14.8 164.1 %reduce-scatter.2.cloned.1.call-start = ((), (), s32[]{:S(2)}) async-start(), calls=%async_computation.3 | async-start | bytes 4456448 | tf_op jit(solution)/shard_map/reduce_scatter | solution.py:33
Sparse Core Ops, SparseCore 0:
  107.0 71.8 reduce-scatter.1
where the time goes:
time: 190 us; the launch traced here: 187 us
  waiting for transfers between devices  72 us (38%)
  blocking collectives  26.6 us (14%)
  matrix products  26.1 us (14%)
  local copies, waits for them, and re-layouts  25.8 us (14%)
  other arithmetic  17.1 us (9%)
  between operations  13.5 us (7%)
  starting transfers between devices  6.33 us (3%)
    reduce_scatter x1, waiting for transfers between devices, body(): lax.psum_scatter(lax.dot_general(down_weight, rotated, (((0,), (1,)), (()...  72 us
    all_to_all x1, blocking collectives, body(): lax.all_to_all(gathered, 'tensor', split_axis=1, concat_axis=0, tiled=True)  26.6 us
    mul x1, local copies, waits for them, and re-layouts, body(): kronecker = jnp.kron(sylvester(span), rotation_small)  25.8 us
    dot_general x1, matrix products, body(): lax.dot_general(down_weight, rotated, (((0,), (1,)), ((), ())), preferred...  14.7 us
    mul x1, other arithmetic, body(): kronecker = jnp.kron(sylvester(span), rotation_small)  13.3 us
    dot_general x1, matrix products, body(): jnp.dot(gathered.reshape(-1, local), kronecker, precision=lax.Precision.H...  10.5 us
    all_to_all x1, starting transfers between devices, body(): lax.all_to_all(values, 'tensor', split_axis=0, concat_axis=1, tiled=True)  6.3 us
  transfers between devices with their start and end apart: 2, of which 1 were waited for; matrix products, arithmetic and copies ran while one was open for 21% of the time, Pallas kernels for 0%

commit v1 on v0

--- a/solution.py
+++ b/solution.py
@@ -1,9 +1,15 @@
+import functools
+
 import jax
 import jax.numpy as jnp
 from jax import lax
+from jax.experimental import pallas as pl
+from jax.experimental.pallas import tpu as pltpu
 from jax.sharding import PartitionSpec as P
 
-BLOCK = 52
+LANES = 128
+ROWS = 8
+SPLIT = 2
 
 
 def sylvester(order):
@@ -14,10 +20,10 @@
     return (1 - 2 * (common % 2)).astype(jnp.float32)
 
 
-def body(activations, rotation_small, down_weight):
+def plain(activations, rotation_small, down_weight):
     tokens, local = activations.shape
     shards = lax.axis_size("tensor")
-    span = local // BLOCK
+    span = local // rotation_small.shape[0]
     kronecker = jnp.kron(sylvester(span), rotation_small)
     factor = (span * shards) ** (-0.5)
     values = activations.astype(jnp.float32)
@@ -41,6 +47,300 @@
     return summed.T.astype(jnp.bfloat16)
 
 
+def widths_of(tiles):
+    chunks = min(4, tiles)
+    sizes = [tiles // chunks] * chunks
+    for extra in range(tiles % chunks):
+        sizes[(1 + extra) % chunks] += 1
+    return [size * LANES for size in sizes]
+
+
+def ends_first(count):
+    low, high, order = 0, count - 1, []
+    while low <= high:
+        order.append(high)
+        if low < high:
+            order.append(low)
+        low, high = low + 1, high - 1
+    return order
+
+
+def fused(n, widths, act, small, w_hbm, out, w_v, acc, *rest):
+    chunks = len(widths)
+    own, got, mixed, back = (rest[i * chunks : (i + 1) * chunks] for i in range(4))
+    (from_core, from_y, from_low, from_high, w_sem, s1, r1, s2, r2, sa, ra, sb, rb,
+     su, ru, sd, rd) = rest[4 * chunks :]
+    tokens, local = act.shape
+    block = small.shape[0]
+    width = acc.shape[2]
+    rows = tokens // n
+    part = tokens // SPLIT
+    nz = n // 4
+    me = lax.axis_index("tensor")
+    z, y, c = me // 4, (me // 2) % 2, me % 2
+    starts = [sum(widths[:j]) for j in range(chunks)]
+    scale = (local // block * n) ** (-0.5)
+
+    def w_copy(j):
+        span = pl.ds(starts[j], widths[j])
+        return pltpu.make_async_copy(w_hbm.at[span], w_v.at[span], w_sem.at[j])
+
+    for j in range(chunks):
+        w_copy(j).start()
+
+    barrier = pltpu.get_barrier_semaphore()
+
+    def greet(k, carry):
+        pl.semaphore_signal(barrier, inc=1, device_id={"tensor": lax.rem(me + k, n)})
+        return carry
+
+    lax.fori_loop(1, n, greet, 0)
+
+    def remote(src, dst, send, recv, to):
+        return pltpu.make_async_remote_copy(
+            src_ref=src, dst_ref=dst, send_sem=send, recv_sem=recv,
+            device_id={"tensor": to}, device_id_type=pl.DeviceIdType.MESH,
+        )
+
+    def rows_of(rank):
+        return pl.ds(pl.multiple_of(rank * rows, ROWS), rows)
+
+    def out_copy(j, k):
+        to = lax.rem(me + k, n)
+        return remote(own[j].at[rows_of(to)], got[j].at[me], s1.at[j, k], r1.at[j, k], to)
+
+    def back_copy(j, k):
+        to = lax.rem(me + k, n)
+        return remote(mixed[j].at[to], back[j].at[rows_of(me)], s2.at[j, k], r2.at[j, k], to)
+
+    def each(action):
+        def step(k, carry):
+            action(k)
+            return carry
+
+        lax.fori_loop(1, n, step, 0)
+
+    def split_index(index):
+        whole = jnp.floor((index.astype(jnp.float32) + 0.5) * (1.0 / block))
+        whole = whole.astype(jnp.int32)
+        return whole, index - whole * block
+
+    r = small[...]
+    r_high = r.astype(jnp.bfloat16)
+    r_low = (r - r_high.astype(jnp.float32)).astype(jnp.bfloat16)
+    span = local // block
+
+    def dot(a, b):
+        return jnp.dot(a, b, preferred_element_type=jnp.float32)
+
+    for j, w in enumerate(widths):
+        col_p, col_q = split_index(lax.broadcasted_iota(jnp.int32, (block, w), 1) + starts[j])
+        line = lax.broadcasted_iota(jnp.int32, (block, w), 0)
+        pick = jnp.where(col_q == line, 1.0, 0.0).astype(jnp.bfloat16)
+        right_high = dot(r_high, pick).astype(jnp.bfloat16)
+        right_low = dot(r_low, pick).astype(jnp.bfloat16)
+        odd = jnp.zeros_like(line)
+        for place in range(span.bit_length()):
+            odd = odd + ((line >> place) & 1) * ((col_p >> place) & 1)
+        sign_right = jnp.where(line < span, (1 - 2 * (odd & 1)).astype(jnp.float32), 0.0)
+        sign_right = sign_right.astype(jnp.bfloat16)
+        own[j][...] = jnp.zeros_like(own[j])
+
+        def build(i, carry):
+            base = pl.multiple_of(i * LANES, LANES)
+            row_p, row_q = split_index(lax.broadcasted_iota(jnp.int32, (LANES, block), 0) + base)
+            lane = lax.broadcasted_iota(jnp.int32, (LANES, block), 1)
+            left = jnp.where(row_q == lane, 1.0, 0.0).astype(jnp.bfloat16)
+            sign = dot(jnp.where(row_p == lane, 1.0, 0.0).astype(jnp.bfloat16), sign_right)
+            high = (dot(left, right_high) * sign).astype(jnp.bfloat16)
+            low = (dot(left, right_low) * sign).astype(jnp.bfloat16)
+            x = act[:, pl.ds(base, LANES)]
+            own[j][...] += dot(x, high) + dot(x, low)
+            return carry
+
+        lax.fori_loop(0, local // LANES, build, 0)
+        if j == 0:
+            pl.semaphore_wait(barrier, n - 1)
+        each(lambda k: out_copy(j, k).start())
+        got[j][me] = own[j][rows_of(me), :]
+
+    for j, w in enumerate(widths):
+        each(lambda k: out_copy(j, k).wait_recv())
+        for at in range(0, w, LANES):
+            values = [got[j][s, :, at : at + LANES] for s in range(n)]
+            stride = 1
+            while stride < n:
+                for low in range(n):
+                    if not low & stride:
+                        a, b = values[low], values[low + stride]
+                        values[low], values[low + stride] = a + b, a - b
+                stride *= 2
+            for s in range(n):
+                mixed[j][s, :, at : at + LANES] = values[s] * scale
+        each(lambda k: back_copy(j, k).start())
+        back[j][rows_of(me), :] = mixed[j][me]
+
+    def product(j, t):
+        columns = pl.ds(pl.multiple_of(t * width, LANES), width)
+        weight = w_v[pl.ds(starts[j], widths[j]), columns]
+        return dot(back[j][...].astype(jnp.bfloat16), weight)
+
+    for j in range(chunks - 1):
+        each(lambda k: back_copy(j, k).wait_recv())
+        w_copy(j).wait()
+
+        def tile(t, carry):
+            if j == 0:
+                acc[t] = product(j, t)
+            else:
+                acc[t] += product(j, t)
+            return carry
+
+        lax.fori_loop(0, n, tile, 0)
+
+    last = chunks - 1
+    each(lambda k: back_copy(last, k).wait_recv())
+    w_copy(last).wait()
+
+    order = ends_first(nz)
+    slots = [(far, to) for far in (1, 0) for to in order]
+
+    def owner(to, far, other):
+        side = 1 - y if far else y
+        return to * 4 + side * 2 + (1 - c if other else c)
+
+    def core_copy(slot):
+        far, to = slots[slot]
+        return remote(acc.at[owner(to, far, 1)], from_core.at[slot], sa.at[slot], ra.at[slot],
+                      me + 1 - 2 * c)
+
+    def y_copy(to, h):
+        return remote(acc.at[owner(to, 1, 0), pl.ds(h * part, part)], from_y.at[to, h],
+                      sb.at[to, h], rb.at[to, h], me + 2 * (1 - 2 * y))
+
+    def up_copy(to, h, t):
+        return remote(acc.at[t, pl.ds(h * part, part)], from_low.at[to, h],
+                      su.at[to, h], ru.at[to, h], lax.rem(me + 4, n))
+
+    def down_copy(to, h, t):
+        return remote(acc.at[t, pl.ds(h * part, part)], from_high.at[to, h],
+                      sd.at[to, h], rd.at[to, h], lax.rem(me + n - 4, n))
+
+    for slot, (far, to) in enumerate(slots):
+        t = owner(to, far, 1)
+        acc[t] += product(last, t)
+        core_copy(slot).start()
+    for slot, (far, to) in enumerate(slots):
+        t = owner(to, far, 0)
+        acc[t] += product(last, t)
+        core_copy(slot).wait_recv()
+        acc[t] += from_core[slot]
+        if far:
+            for h in range(SPLIT):
+                y_copy(to, h).start()
+
+    for to in order:
+        t = owner(to, 0, 0)
+        for h in range(SPLIT):
+            piece = pl.ds(h * part, part)
+            y_copy(to, h).wait_recv()
+            acc[t, piece] += from_y[to, h]
+
+            @pl.when(z < to)
+            def _():
+                @pl.when(z > 0)
+                def _():
+                    up_copy(to, h, t).wait_recv()
+                    acc[t, piece] += from_low[to, h]
+
+                up_copy(to, h, t).start()
+
+            @pl.when(z > to)
+            def _():
+                @pl.when(z < nz - 1)
+                def _():
+                    down_copy(to, h, t).wait_recv()
+                    acc[t, piece] += from_high[to, h]
+
+                down_copy(to, h, t).start()
+
+    for h in range(SPLIT):
+        piece = pl.ds(h * part, part)
+
+        @pl.when(z > 0)
+        def _():
+            up_copy(z, h, me).wait_recv()
+            acc[me, piece] += from_low[z, h]
+
+        @pl.when(z < nz - 1)
+        def _():
+            down_copy(z, h, me).wait_recv()
+            acc[me, piece] += from_high[z, h]
+
+        out[piece, :] = acc[me, piece].astype(out.dtype)
+
+    for j in range(chunks):
+        each(lambda k: out_copy(j, k).wait_send())
+        each(lambda k: back_copy(j, k).wait_send())
+    for slot in range(len(slots)):
+        core_copy(slot).wait_send()
+    for to in order:
+        for h in range(SPLIT):
+            y_copy(to, h).wait_send()
+            t = owner(to, 0, 0)
+
+            @pl.when(z < to)
+            def _():
+                up_copy(to, h, t).wait_send()
+
+            @pl.when(z > to)
+            def _():
+                down_copy(to, h, t).wait_send()
+
+
+def body(activations, rotation_small, down_weight):
+    tokens, local = activations.shape
+    n = lax.axis_size("tensor")
+    features = down_weight.shape[1]
+    block = rotation_small.shape[0]
+    if n % 4 or block * block < local or tokens % (ROWS * n) or local % LANES or features % (LANES * n):
+        return plain(activations, rotation_small, down_weight)
+    widths = widths_of(local // LANES)
+    chunks, width, nz, part = len(widths), features // n, n // 4, tokens // SPLIT
+    rows = tokens // n
+    f32 = jnp.float32
+    dma = pltpu.SemaphoreType.DMA
+    return pl.pallas_call(
+        functools.partial(fused, n, widths),
+        out_shape=jax.ShapeDtypeStruct((tokens, width), jnp.bfloat16),
+        in_specs=[
+            pl.BlockSpec(memory_space=pltpu.VMEM),
+            pl.BlockSpec(memory_space=pltpu.VMEM),
+            pl.BlockSpec(memory_space=pl.ANY),
+        ],
+        out_specs=pl.BlockSpec(memory_space=pltpu.VMEM),
+        scratch_shapes=[
+            pltpu.VMEM((local, features), jnp.bfloat16),
+            pltpu.VMEM((n, tokens, width), f32),
+            *[pltpu.VMEM((tokens, w), f32) for w in widths],
+            *[pltpu.VMEM((n, rows, w), f32) for w in widths],
+            *[pltpu.VMEM((n, rows, w), f32) for w in widths],
+            *[pltpu.VMEM((tokens, w), f32) for w in widths],
+            pltpu.VMEM((2 * nz, tokens, width), f32),
+            pltpu.VMEM((nz, SPLIT, part, width), f32),
+            pltpu.VMEM((nz, SPLIT, part, width), f32),
+            pltpu.VMEM((nz, SPLIT, part, width), f32),
+            dma((chunks,)),
+            *[dma((chunks, n))] * 4,
+            *[dma((2 * nz,))] * 2,
+            *[dma((nz, SPLIT))] * 6,
+        ],
+        compiler_params=pltpu.CompilerParams(
+            collective_id=0, has_side_effects=True, vmem_limit_bytes=60 * 2**20
+        ),
+    )(activations, rotation_small, down_weight)
+
+
 def solution(mesh):
     placed = (P("groups", "tensor"), P(), P("tensor", None))
     return jax.shard_map(

time: 190 us -> 95.2 us (0.50); the launches traced: 187 us -> 95.1 us
  Pallas kernels: 0 us -> 93.5 us
  waiting for transfers between devices: 72 us -> 0 us
  blocking collectives: 26.6 us -> 0 us
  matrix products: 26.1 us -> 0 us
  local copies, waits for them, and re-layouts: 25.8 us -> 1.57 us
  other arithmetic: 17.1 us -> 0 us
  between operations: 13.5 us -> 0.01 us
  starting transfers between devices: 6.33 us -> 0 us
    pallas_call x0 -> x1, Pallas kernels: none -> 93.5 us  [body(): pl.pallas_call(functools.partial(fused, n, widths), out_shape=jax.ShapeDt...]
    reduce_scatter x1 -> x0, waiting for transfers between devices: 72 us -> none  [body(): lax.psum_scatter(lax.dot_general(down_weight, rotated, (((0,), (1,)), (()...]
    all_to_all x1 -> x0, blocking collectives: 26.6 us -> none  [body(): lax.all_to_all(gathered, 'tensor', split_axis=1, concat_axis=0, tiled=True)]
    dot_general x3 -> x0, matrix products: 26.1 us -> none  [the longest x1 14.7 us: body(): lax.dot_general(down_weight, rotated, (((0,), (1,)), ((), ())), preferred...]
    mul x1 -> x0, local copies, waits for them, and re-layouts: 25.8 us -> none  [body(): kronecker = jnp.kron(sylvester(span), rotation_small)]
    mul x1 -> x0, other arithmetic: 13.3 us -> none  [body(): kronecker = jnp.kron(sylvester(span), rotation_small)]
    all_to_all x1 -> x0, starting transfers between devices: 6.3 us -> none  [body(): lax.all_to_all(values, 'tensor', split_axis=0, concat_axis=1, tiled=True)]
    all_to_all x1 -> x0, other arithmetic: 1.99 us -> none  [body(): lax.all_to_all(values, 'tensor', split_axis=0, concat_axis=1, tiled=True)]
  transfers between devices with their start and end apart: 2 -> 0, of which waited for: 1 -> 0; matrix products, arithmetic and copies ran while one was open for 21% -> 0% of each run, Pallas kernels for 0% -> 0%
where the time goes in v1:
time: 95.2 us; the launch traced here: 95.1 us
  Pallas kernels  93.5 us (98%)
  local copies, waits for them, and re-layouts  1.57 us (2%)
    pallas_call x1, Pallas kernels, body(): pl.pallas_call(functools.partial(fused, n, widths), out_shape=jax.ShapeDt...  93.5 us

profile of v1, /device:TPU:8, one launch (start us, length us, event | category | flops | bytes accessed | tf_op | source)
XLA Modules:
  0.0 95.1 jit_solution(13766582424303478056)
XLA Ops:
  0.0 93.5 %shard_map.37 = bf16[128,512]{1,0:T(8,128)(2,1)} custom-call(bf16[128,1664]{1,0:T(8,128)(2,1)} %act.1, f32[52,52]{1,0:T(8,128)} %small.1, bf16[1664,8192]{1,0:T(8,128)(2,1)} %w_hbm.1), custom_call_target="tpu_custom_call" | custom-call | tf_op jit(solution)/shard_map/pallas_call | solution.py:313
  93.5 1.6 %copy.5 = bf16[128,512]{1,0:T(8,128)(2,1)} copy(bf16[128,512]{1,0:T(8,128)(2,1)} %shard_map.37) | data formatting | bytes 262144

commit v2 on v1

--- a/solution.py
+++ b/solution.py
@@ -65,11 +65,11 @@
     return order
 
 
-def fused(n, widths, act, small, w_hbm, out, w_v, acc, *rest):
+def fused(n, widths, act, small, w_hbm, out, w_v, acc, pieced, own, *rest):
     chunks = len(widths)
-    own, got, mixed, back = (rest[i * chunks : (i + 1) * chunks] for i in range(4))
+    got, mixed, back = (rest[i * chunks : (i + 1) * chunks] for i in range(3))
     (from_core, from_y, from_low, from_high, w_sem, s1, r1, s2, r2, sa, ra, sb, rb,
-     su, ru, sd, rd) = rest[4 * chunks :]
+     su, ru, sd, rd) = rest[3 * chunks :]
     tokens, local = act.shape
     block = small.shape[0]
     width = acc.shape[2]
@@ -107,7 +107,7 @@
 
     def out_copy(j, k):
         to = lax.rem(me + k, n)
-        return remote(own[j].at[rows_of(to)], got[j].at[me], s1.at[j, k], r1.at[j, k], to)
+        return remote(own.at[rows_of(to), pl.ds(starts[j], widths[j])], got[j].at[me], s1.at[j, k], r1.at[j, k], to)
 
     def back_copy(j, k):
         to = lax.rem(me + k, n)
@@ -133,48 +133,54 @@
     def dot(a, b):
         return jnp.dot(a, b, preferred_element_type=jnp.float32)
 
-    for j, w in enumerate(widths):
-        col_p, col_q = split_index(lax.broadcasted_iota(jnp.int32, (block, w), 1) + starts[j])
-        line = lax.broadcasted_iota(jnp.int32, (block, w), 0)
-        pick = jnp.where(col_q == line, 1.0, 0.0).astype(jnp.bfloat16)
-        right_high = dot(r_high, pick).astype(jnp.bfloat16)
-        right_low = dot(r_low, pick).astype(jnp.bfloat16)
-        odd = jnp.zeros_like(line)
-        for place in range(span.bit_length()):
-            odd = odd + ((line >> place) & 1) * ((col_p >> place) & 1)
-        sign_right = jnp.where(line < span, (1 - 2 * (odd & 1)).astype(jnp.float32), 0.0)
-        sign_right = sign_right.astype(jnp.bfloat16)
-        own[j][...] = jnp.zeros_like(own[j])
-
-        def build(i, carry):
-            base = pl.multiple_of(i * LANES, LANES)
-            row_p, row_q = split_index(lax.broadcasted_iota(jnp.int32, (LANES, block), 0) + base)
-            lane = lax.broadcasted_iota(jnp.int32, (LANES, block), 1)
-            left = jnp.where(row_q == lane, 1.0, 0.0).astype(jnp.bfloat16)
-            sign = dot(jnp.where(row_p == lane, 1.0, 0.0).astype(jnp.bfloat16), sign_right)
-            high = (dot(left, right_high) * sign).astype(jnp.bfloat16)
-            low = (dot(left, right_low) * sign).astype(jnp.bfloat16)
-            x = act[:, pl.ds(base, LANES)]
-            own[j][...] += dot(x, high) + dot(x, low)
-            return carry
-
-        lax.fori_loop(0, local // LANES, build, 0)
-        if j == 0:
-            pl.semaphore_wait(barrier, n - 1)
+    pieces, _, pw = pieced.shape
+    inner = span // pieces
+
+    def grid_of(shape, dim):
+        return split_index(lax.broadcasted_iota(jnp.int32, shape, dim))
+
+    def one_hot(hit):
+        return jnp.where(hit, 1.0, 0.0).astype(jnp.bfloat16)
+
+    col_p, col_q = grid_of((block, pw), 1)
+    line = lax.broadcasted_iota(jnp.int32, (block, pw), 0)
+    pick = one_hot(col_q == line)
+    odd = jnp.zeros_like(line)
+    for place in range(inner.bit_length()):
+        odd = odd + ((line >> place) & 1) * ((col_p >> place) & 1)
+    sign_right = jnp.where(line < inner, (1 - 2 * (odd & 1)).astype(jnp.float32), 0.0)
+    row_p, row_q = grid_of((pw, block), 0)
+    lane = lax.broadcasted_iota(jnp.int32, (pw, block), 1)
+    left = one_hot(row_q == lane)
+    sign = dot(one_hot(row_p == lane), sign_right.astype(jnp.bfloat16))
+    high = (dot(left, dot(r_high, pick).astype(jnp.bfloat16)) * sign).astype(jnp.bfloat16)
+    low = (dot(left, dot(r_low, pick).astype(jnp.bfloat16)) * sign).astype(jnp.bfloat16)
+    for i in range(pieces):
+        x = act[:, i * pw : (i + 1) * pw]
+        pieced[i] = dot(x, high) + dot(x, low)
+
+    def butterfly(values):
+        stride = 1
+        while stride < len(values):
+            for at in range(len(values)):
+                if not at & stride:
+                    a, b = values[at], values[at + stride]
+                    values[at], values[at + stride] = a + b, a - b
+            stride *= 2
+        return values
+
+    for at in range(0, tokens, ROWS):
+        values = butterfly([pieced[i, at : at + ROWS, :] for i in range(pieces)])
+        own[at : at + ROWS, :] = jnp.concatenate(values, axis=1)
+    pl.semaphore_wait(barrier, n - 1)
+    for j in range(chunks):
         each(lambda k: out_copy(j, k).start())
-        got[j][me] = own[j][rows_of(me), :]
+        got[j][me] = own[rows_of(me), pl.ds(starts[j], widths[j])]
 
     for j, w in enumerate(widths):
         each(lambda k: out_copy(j, k).wait_recv())
         for at in range(0, w, LANES):
-            values = [got[j][s, :, at : at + LANES] for s in range(n)]
-            stride = 1
-            while stride < n:
-                for low in range(n):
-                    if not low & stride:
-                        a, b = values[low], values[low + stride]
-                        values[low], values[low + stride] = a + b, a - b
-                stride *= 2
+            values = butterfly([got[j][s, :, at : at + LANES] for s in range(n)])
             for s in range(n):
                 mixed[j][s, :, at : at + LANES] = values[s] * scale
         each(lambda k: back_copy(j, k).start())
@@ -308,6 +314,9 @@
     widths = widths_of(local // LANES)
     chunks, width, nz, part = len(widths), features // n, n // 4, tokens // SPLIT
     rows = tokens // n
+    pieces = 1
+    while local // pieces > 2 * LANES and local // block % (2 * pieces) == 0:
+        pieces *= 2
     f32 = jnp.float32
     dma = pltpu.SemaphoreType.DMA
     return pl.pallas_call(
@@ -322,7 +331,8 @@
         scratch_shapes=[
             pltpu.VMEM((local, features), jnp.bfloat16),
             pltpu.VMEM((n, tokens, width), f32),
-            *[pltpu.VMEM((tokens, w), f32) for w in widths],
+            pltpu.VMEM((pieces, tokens, local // pieces), f32),
+            pltpu.VMEM((tokens, local), f32),
             *[pltpu.VMEM((n, rows, w), f32) for w in widths],
             *[pltpu.VMEM((n, rows, w), f32) for w in widths],
             *[pltpu.VMEM((tokens, w), f32) for w in widths],

time: 95.2 us -> 90.5 us (0.951)
  Pallas kernels: 93.5 us -> 88.7 us
    pallas_call x1, Pallas kernels: 93.5 us -> 88.7 us  [body(): pl.pallas_call(functools.partial(fused, n, widths), out_shape=jax.ShapeDt...]
where the time goes in v2:
time: 90.5 us; the launch traced here: 90.3 us
  Pallas kernels  88.7 us (98%)
  local copies, waits for them, and re-layouts  1.57 us (2%)
    pallas_call x1, Pallas kernels, body(): pl.pallas_call(functools.partial(fused, n, widths), out_shape=jax.ShapeDt...  88.7 us

profile of v2, /device:TPU:8, one launch (start us, length us, event | category | flops | bytes accessed | tf_op | source)
XLA Modules:
  0.0 90.3 jit_solution(206463126562396383)
XLA Ops:
  0.0 88.7 %shard_map.37 = bf16[128,512]{1,0:T(8,128)(2,1)} custom-call(bf16[128,1664]{1,0:T(8,128)(2,1)} %act.1, f32[52,52]{1,0:T(8,128)} %small.1, bf16[1664,8192]{1,0:T(8,128)(2,1)} %w_hbm.1), custom_call_target="tpu_custom_call" | custom-call | tf_op jit(solution)/shard_map/pallas_call | solution.py:322
  88.7 1.6 %copy.5 = bf16[128,512]{1,0:T(8,128)(2,1)} copy(bf16[128,512]{1,0:T(8,128)(2,1)} %shard_map.37) | data formatting | bytes 262144

commit v3 on v2

v3 whole, which is shorter than its diff:
```python
import functools

import jax
import jax.numpy as jnp
from jax import lax
from jax.experimental import pallas as pl
from jax.experimental.pallas import tpu as pltpu
from jax.sharding import PartitionSpec as P

LANES = 128
ROWS = 8
SPLIT = 2


def sylvester(order):
    index = jnp.arange(order, dtype=jnp.int32)
    common = jnp.zeros((order, order), jnp.int32)
    for place in range(max(order.bit_length(), 1)):
        common = common + (index[:, None] >> place & 1) * (index[None, :] >> place & 1)
    return (1 - 2 * (common % 2)).astype(jnp.float32)


def plain(activations, rotation_small, down_weight):
    tokens, local = activations.shape
    shards = lax.axis_size("tensor")
    span = local // rotation_small.shape[0]
    kronecker = jnp.kron(sylvester(span), rotation_small)
    factor = (span * shards) ** (-0.5)
    values = activations.astype(jnp.float32)
    gathered = lax.all_to_all(values, "tensor", split_axis=0, concat_axis=1, tiled=True)
    gathered = gathered.reshape(-1, shards, local)
    gathered = jnp.einsum(
        "rsl,su->rul", gathered, sylvester(shards), precision=lax.Precision.HIGHEST
    )
    gathered = jnp.dot(gathered.reshape(-1, local), kronecker, precision=lax.Precision.HIGHEST)
    gathered = gathered.reshape(-1, shards * local)
    returned = lax.all_to_all(gathered, "tensor", split_axis=1, concat_axis=0, tiled=True)
    rotated = (returned * factor).astype(jnp.bfloat16)
    summed = lax.psum_scatter(
        lax.dot_general(
            down_weight, rotated, (((0,), (1,)), ((), ())), preferred_element_type=jnp.float32
        ),
        "tensor",
        scatter_dimension=0,
        tiled=True,
    )
    return summed.T.astype(jnp.bfloat16)


def ends_first(count):
    low, high, order = 0, count - 1, []
    while low <= high:
        order.append(high)
        if low < high:
            order.append(low)
        low, high = low + 1, high - 1
    return order


def fused(n, act, small, w_hbm, out, w_v, acc, pieced, own, got, mixed, back, rotated, from_core,
          from_y, from_low, from_high, w_sem, s1, r1, s2, r2, sa, ra, sb, rb, su, ru, sd, rd):
    tokens, local = act.shape
    block = small.shape[0]
    width = acc.shape[3]
    part = tokens // SPLIT
    rows = part // (n // 2)
    wide = got.shape[3]
    shift = local - wide
    nz = n // 4
    me = lax.axis_index("tensor")
    z, y, c = me // 4, (me // 2) % 2, me % 2
    scale = (local // block * n) ** (-0.5)
    w_copy = pltpu.make_async_copy(w_hbm, w_v, w_sem)
    w_copy.start()

    barrier = pltpu.get_barrier_semaphore()

    def greet(k, carry):
        pl.semaphore_signal(barrier, inc=1, device_id={"tensor": lax.rem(me + k, n)})
        return carry

    lax.fori_loop(1, n, greet, 0)

    def remote(src, dst, send, recv, to):
        return pltpu.make_async_remote_copy(
            src_ref=src, dst_ref=dst, send_sem=send, recv_sem=recv,
            device_id={"tensor": to}, device_id_type=pl.DeviceIdType.MESH,
        )

    def rows_of(rank, base=0):
        return pl.ds(pl.multiple_of(base + rank // 2 * rows, ROWS), rows)

    def columns_of(rank):
        return pl.ds(pl.multiple_of(rank % 2 * shift, LANES), wide)

    def out_copy(h, k):
        to = lax.rem(me + k, n)
        return remote(own.at[rows_of(to, h * part), columns_of(to)], got.at[h, me],
                      s1.at[h, k], r1.at[h, k], to)

    def back_copy(h, k):
        to = lax.rem(me + k, n)
        return remote(mixed.at[h, to], back.at[h, c, rows_of(me)], s2.at[h, k], r2.at[h, k], to)

    def each(action):
        def step(k, carry):
            action(k)
            return carry

        lax.fori_loop(1, n, step, 0)

    def split_index(index):
        whole = jnp.floor((index.astype(jnp.float32) + 0.5) * (1.0 / block))
        whole = whole.astype(jnp.int32)
        return whole, index - whole * block

    r = small[...]
    r_high = r.astype(jnp.bfloat16)
    r_low = (r - r_high.astype(jnp.float32)).astype(jnp.bfloat16)
    span = local // block

    def dot(a, b):
        return jnp.dot(a, b, preferred_element_type=jnp.float32)

    pieces, _, pw = pieced.shape
    inner = span // pieces

    def grid_of(shape, dim):
        return split_index(lax.broadcasted_iota(jnp.int32, shape, dim))

    def one_hot(hit):
        return jnp.where(hit, 1.0, 0.0).astype(jnp.bfloat16)

    col_p, col_q = grid_of((block, pw), 1)
    line = lax.broadcasted_iota(jnp.int32, (block, pw), 0)
    pick = one_hot(col_q == line)
    odd = jnp.zeros_like(line)
    for place in range(inner.bit_length()):
        odd = odd + ((line >> place) & 1) * ((col_p >> place) & 1)
    sign_right = jnp.where(line < inner, (1 - 2 * (odd & 1)).astype(jnp.float32), 0.0)
    row_p, row_q = grid_of((pw, block), 0)
    lane = lax.broadcasted_iota(jnp.int32, (pw, block), 1)
    left = one_hot(row_q == lane)
    sign = dot(one_hot(row_p == lane), sign_right.astype(jnp.bfloat16))
    high = (dot(left, dot(r_high, pick).astype(jnp.bfloat16)) * sign).astype(jnp.bfloat16)
    low = (dot(left, dot(r_low, pick).astype(jnp.bfloat16)) * sign).astype(jnp.bfloat16)
    for i in range(pieces):
        x = act[:, i * pw : (i + 1) * pw]
        pieced[i] = dot(x, high) + dot(x, low)

    def butterfly(values):
        stride = 1
        while stride < len(values):
            for at in range(len(values)):
                if not at & stride:
                    a, b = values[at], values[at + stride]
                    values[at], values[at + stride] = a + b, a - b
            stride *= 2
        return values

    for at in range(0, tokens, ROWS):
        values = butterfly([pieced[i, at : at + ROWS, :] for i in range(pieces)])
        own[at : at + ROWS, :] = jnp.concatenate(values, axis=1)
    pl.semaphore_wait(barrier, n - 1)
    for h in range(SPLIT):
        each(lambda k: out_copy(h, k).start())
        got[h, me] = own[rows_of(me, h * part), columns_of(me)]

    for h in range(SPLIT):
        each(lambda k: out_copy(h, k).wait_recv())
        for at in range(0, wide, LANES):
            for low in range(0, rows, ROWS):
                spot = (slice(low, low + ROWS), slice(at, at + LANES))
                values = butterfly([got[(h, s, *spot)] for s in range(n)])
                for s in range(n):
                    mixed[(h, s, *spot)] = values[s] * scale
        each(lambda k: back_copy(h, k).start())
        back[h, c, rows_of(me), :] = mixed[h, me]

    order = ends_first(nz)

    def place_of(i):
        return (1 - i % 2) * (nz - 1 - i // 2) + i % 2 * (i // 2)

    def owner(to, far, other):
        side = 1 - y if far else y
        return to * 4 + side * 2 + (1 - c if other else c)

    def core_copy(h, i, far):
        slot = (1 - far) * nz + i
        return remote(acc.at[h, owner(place_of(i), far, 1)], from_core.at[h, slot],
                      sa.at[h, slot], ra.at[h, slot], me + 1 - 2 * c)

    def y_copy(to, h):
        return remote(acc.at[h, owner(to, 1, 0)], from_y.at[to, h],
                      sb.at[to, h], rb.at[to, h], me + 2 * (1 - 2 * y))

    def up_copy(to, h, t):
        return remote(acc.at[h, t], from_low.at[to, h],
                      su.at[to, h], ru.at[to, h], lax.rem(me + 4, n))

    def down_copy(to, h, t):
        return remote(acc.at[h, t], from_high.at[to, h],
                      sd.at[to, h], rd.at[to, h], lax.rem(me + n - 4, n))

    def product(h, t):
        columns = pl.ds(pl.multiple_of(t * width, LANES), width)
        acc[h, t] = dot(rotated[h], w_v[:, columns])

    def loop(action):
        def step(i, carry):
            action(i)
            return carry

        lax.fori_loop(0, nz, step, 0)

    for h in range(SPLIT):
        each(lambda k: back_copy(h, k).wait_recv())
        rotated[h, :, :wide] = back[h, 0].astype(jnp.bfloat16)
        rotated[h, :, wide:] = back[h, 1, :, wide - shift :].astype(jnp.bfloat16)
        if h == 0:
            w_copy.wait()
        for far in (1, 0):
            def give(i):
                product(h, owner(place_of(i), far, 1))
                core_copy(h, i, far).start()

            loop(give)
        for far in (1, 0):
            def take(i):
                t = owner(place_of(i), far, 0)
                product(h, t)
                core_copy(h, i, far).wait_recv()
                acc[h, t] += from_core[h, (1 - far) * nz + i]
                if far:
                    y_copy(place_of(i), h).start()

            loop(take)

    for h in range(SPLIT):
        for to in order:
            t = owner(to, 0, 0)
            y_copy(to, h).wait_recv()
            acc[h, t] += from_y[to, h]

            @pl.when(z < to)
            def _():
                @pl.when(z > 0)
                def _():
                    up_copy(to, h, t).wait_recv()
                    acc[h, t] += from_low[to, h]

                up_copy(to, h, t).start()

            @pl.when(z > to)
            def _():
                @pl.when(z < nz - 1)
                def _():
                    down_copy(to, h, t).wait_recv()
                    acc[h, t] += from_high[to, h]

                down_copy(to, h, t).start()

    for h in range(SPLIT):
        @pl.when(z > 0)
        def _():
            up_copy(z, h, me).wait_recv()
            acc[h, me] += from_low[z, h]

        @pl.when(z < nz - 1)
        def _():
            down_copy(z, h, me).wait_recv()
            acc[h, me] += from_high[z, h]

        out[h * part : (h + 1) * part, :] = acc[h, me].astype(out.dtype)

    for h in range(SPLIT):
        each(lambda k: out_copy(h, k).wait_send())
        each(lambda k: back_copy(h, k).wait_send())
        for far in (1, 0):
            loop(lambda i: core_copy(h, i, far).wait_send())
        for to in order:
            t = owner(to, 0, 0)
            y_copy(to, h).wait_send()

            @pl.when(z < to)
            def _():
                up_copy(to, h, t).wait_send()

            @pl.when(z > to)
            def _():
                down_copy(to, h, t).wait_send()


def body(activations, rotation_small, down_weight):
    tokens, local = activations.shape
    n = lax.axis_size("tensor")
    features = down_weight.shape[1]
    block = rotation_small.shape[0]
    if n % 4 or block * block < local or tokens % (SPLIT * ROWS * (n // 2)) or local % LANES or features % (LANES * n):
        return plain(activations, rotation_small, down_weight)
    width, nz, part = features // n, n // 4, tokens // SPLIT
    rows = part // (n // 2)
    wide = -(-local // (2 * LANES)) * LANES
    pieces = 1
    while local // pieces > 2 * LANES and local // block % (2 * pieces) == 0:
        pieces *= 2
    f32 = jnp.float32
    dma = pltpu.SemaphoreType.DMA
    return pl.pallas_call(
        functools.partial(fused, n),
        out_shape=jax.ShapeDtypeStruct((tokens, width), jnp.bfloat16),
        in_specs=[
            pl.BlockSpec(memory_space=pltpu.VMEM),
            pl.BlockSpec(memory_space=pltpu.VMEM),
            pl.BlockSpec(memory_space=pl.ANY),
        ],
        out_specs=pl.BlockSpec(memory_space=pltpu.VMEM),
        scratch_shapes=[
            pltpu.VMEM((local, features), jnp.bfloat16),
            pltpu.VMEM((SPLIT, n, part, width), f32),
            pltpu.VMEM((pieces, tokens, local // pieces), f32),
            pltpu.VMEM((tokens, local), f32),
            pltpu.VMEM((SPLIT, n, rows, wide), f32),
            pltpu.VMEM((SPLIT, n, rows, wide), f32),
            pltpu.VMEM((SPLIT, 2, part, wide), f32),
            pltpu.VMEM((SPLIT, part, local), jnp.bfloat16),
            pltpu.VMEM((SPLIT, 2 * nz, part, width), f32),
            *[pltpu.VMEM((nz, SPLIT, part, width), f32)] * 3,
            dma(()),
            *[dma((SPLIT, n))] * 4,
            *[dma((SPLIT, 2 * nz))] * 2,
            *[dma((nz, SPLIT))] * 6,
        ],
        compiler_params=pltpu.CompilerParams(
            collective_id=0, has_side_effects=True, vmem_limit_bytes=60 * 2**20
        ),
    )(activations, rotation_small, down_weight)


def solution(mesh):
    placed = (P("groups", "tensor"), P(), P("tensor", None))
    return jax.shard_map(
        body, mesh=mesh, in_specs=placed, out_specs=P("groups", "tensor"), check_vma=False
    )
```

time: 90.5 us -> 85.2 us (0.941); the launches traced: 90.3 us -> 83.5 us
  Pallas kernels: 88.7 us -> 82 us
    pallas_call x1, Pallas kernels: 88.7 us -> 82 us  [body(): pl.pallas_call(functools.partial(fused, n), out_shape=jax.ShapeDtypeStruc...]
where the time goes in v3:
time: 85.2 us; the launch traced here: 83.5 us
  Pallas kernels  82 us (96%)
  local copies, waits for them, and re-layouts  1.57 us (2%)
    pallas_call x1, Pallas kernels, body(): pl.pallas_call(functools.partial(fused, n), out_shape=jax.ShapeDtypeStruc...  82 us

profile of v3, /device:TPU:8, one launch (start us, length us, event | category | flops | bytes accessed | tf_op | source)
XLA Modules:
  0.0 83.5 jit_solution(8610532655767591352)
XLA Ops:
  0.0 82.0 %shard_map.37 = bf16[128,512]{1,0:T(8,128)(2,1)} custom-call(bf16[128,1664]{1,0:T(8,128)(2,1)} %act.1, f32[52,52]{1,0:T(8,128)} %small.1, bf16[1664,8192]{1,0:T(8,128)(2,1)} %w_hbm.1), custom_call_target="tpu_custom_call" | custom-call | tf_op jit(solution)/shard_map/pallas_call | solution.py:310
  82.0 1.6 %copy.5 = bf16[128,512]{1,0:T(8,128)(2,1)} copy(bf16[128,512]{1,0:T(8,128)(2,1)} %shard_map.37) | data formatting | bytes 262144

commit v4 on v3

--- a/solution.py
+++ b/solution.py
@@ -90,17 +90,23 @@
     def rows_of(rank, base=0):
         return pl.ds(pl.multiple_of(base + rank // 2 * rows, ROWS), rows)
 
-    def columns_of(rank):
-        return pl.ds(pl.multiple_of(rank % 2 * shift, LANES), wide)
-
-    def out_copy(h, k):
+    overlap = wide - shift
+    first = -(-wide // (2 * LANES)) * LANES
+    cuts = ((0, first), (first, wide - first))
+
+    def columns_of(rank, q):
+        return pl.ds(pl.multiple_of(rank % 2 * shift + cuts[q][0], LANES), cuts[q][1])
+
+    def out_copy(h, q, k):
         to = lax.rem(me + k, n)
-        return remote(own.at[rows_of(to, h * part), columns_of(to)], got.at[h, me],
-                      s1.at[h, k], r1.at[h, k], to)
-
-    def back_copy(h, k):
+        return remote(own.at[rows_of(to, h * part), columns_of(to, q)],
+                      got.at[h, me, :, pl.ds(*cuts[q])], s1.at[h, q, k], r1.at[h, q, k], to)
+
+    def back_copy(h, q, k):
         to = lax.rem(me + k, n)
-        return remote(mixed.at[h, to], back.at[h, c, rows_of(me)], s2.at[h, k], r2.at[h, k], to)
+        return remote(mixed.at[h, to, :, pl.ds(*cuts[q])],
+                      back.at[h, c, rows_of(me), pl.ds(*cuts[q])],
+                      s2.at[h, q, k], r2.at[h, q, k], to)
 
     def each(action):
         def step(k, carry):
@@ -162,20 +168,21 @@
         values = butterfly([pieced[i, at : at + ROWS, :] for i in range(pieces)])
         own[at : at + ROWS, :] = jnp.concatenate(values, axis=1)
     pl.semaphore_wait(barrier, n - 1)
-    for h in range(SPLIT):
-        each(lambda k: out_copy(h, k).start())
-        got[h, me] = own[rows_of(me, h * part), columns_of(me)]
-
-    for h in range(SPLIT):
-        each(lambda k: out_copy(h, k).wait_recv())
-        for at in range(0, wide, LANES):
+    stages = [(h, q) for h in range(SPLIT) for q in range(2)]
+    for h, q in stages:
+        each(lambda k: out_copy(h, q, k).start())
+        got[h, me, :, pl.ds(*cuts[q])] = own[rows_of(me, h * part), columns_of(me, q)]
+
+    for h, q in stages:
+        each(lambda k: out_copy(h, q, k).wait_recv())
+        for at in range(cuts[q][0], sum(cuts[q]), LANES):
             for low in range(0, rows, ROWS):
                 spot = (slice(low, low + ROWS), slice(at, at + LANES))
                 values = butterfly([got[(h, s, *spot)] for s in range(n)])
                 for s in range(n):
                     mixed[(h, s, *spot)] = values[s] * scale
-        each(lambda k: back_copy(h, k).start())
-        back[h, c, rows_of(me), :] = mixed[h, me]
+        each(lambda k: back_copy(h, q, k).start())
+        back[h, c, rows_of(me), pl.ds(*cuts[q])] = mixed[h, me, :, pl.ds(*cuts[q])]
 
     order = ends_first(nz)
 
@@ -203,63 +210,92 @@
         return remote(acc.at[h, t], from_high.at[to, h],
                       sd.at[to, h], rd.at[to, h], lax.rem(me + n - 4, n))
 
-    def product(h, t):
+    def spans(q):
+        at, size = cuts[q]
+        low = max(at, overlap)
+        return (0, at, size), (1, low, at + size - low)
+
+    def receive(h, q):
+        each(lambda k: back_copy(h, q, k).wait_recv())
+        for side, at, size in spans(q):
+            rotated[h, :, pl.ds(side * shift + at, size)] = (
+                back[h, side, :, pl.ds(at, size)].astype(jnp.bfloat16)
+            )
+
+    def product(h, q, t):
         columns = pl.ds(pl.multiple_of(t * width, LANES), width)
-        acc[h, t] = dot(rotated[h], w_v[:, columns])
-
-    def loop(action):
+        terms = [
+            dot(rotated[h, :, pl.ds(side * shift + at, size)],
+                w_v[pl.ds(side * shift + at, size), columns])
+            for side, at, size in spans(q)
+        ]
+        return terms[0] + terms[1]
+
+    def loop(count, action):
         def step(i, carry):
             action(i)
             return carry
 
-        lax.fori_loop(0, nz, step, 0)
-
-    for h in range(SPLIT):
-        each(lambda k: back_copy(h, k).wait_recv())
-        rotated[h, :, :wide] = back[h, 0].astype(jnp.bfloat16)
-        rotated[h, :, wide:] = back[h, 1, :, wide - shift :].astype(jnp.bfloat16)
+        lax.fori_loop(0, count, step, 0)
+
+    def begin(h):
+        receive(h, 0)
         if h == 0:
             w_copy.wait()
-        for far in (1, 0):
-            def give(i):
-                product(h, owner(place_of(i), far, 1))
-                core_copy(h, i, far).start()
-
-            loop(give)
-        for far in (1, 0):
-            def take(i):
-                t = owner(place_of(i), far, 0)
-                product(h, t)
-                core_copy(h, i, far).wait_recv()
-                acc[h, t] += from_core[h, (1 - far) * nz + i]
-                if far:
-                    y_copy(place_of(i), h).start()
-
-            loop(take)
+
+        def tile(t):
+            acc[h, t] = product(h, 0, t)
+
+        loop(n, tile)
+        receive(h, 1)
+
+    def give(h, far, i):
+        t = owner(place_of(i), far, 1)
+        acc[h, t] += product(h, 1, t)
+        core_copy(h, i, far).start()
+
+    def take(h, far, i):
+        t = owner(place_of(i), far, 0)
+        acc[h, t] += product(h, 1, t)
+        core_copy(h, i, far).wait_recv()
+        acc[h, t] += from_core[h, (1 - far) * nz + i]
+        if far:
+            y_copy(place_of(i), h).start()
+
+    def pass_on(h, to):
+        t = owner(to, 0, 0)
+        y_copy(to, h).wait_recv()
+        acc[h, t] += from_y[to, h]
+
+        @pl.when(z < to)
+        def _():
+            @pl.when(z > 0)
+            def _():
+                up_copy(to, h, t).wait_recv()
+                acc[h, t] += from_low[to, h]
+
+            up_copy(to, h, t).start()
+
+        @pl.when(z > to)
+        def _():
+            @pl.when(z < nz - 1)
+            def _():
+                down_copy(to, h, t).wait_recv()
+                acc[h, t] += from_high[to, h]
+
+            down_copy(to, h, t).start()
 
     for h in range(SPLIT):
-        for to in order:
-            t = owner(to, 0, 0)
-            y_copy(to, h).wait_recv()
-            acc[h, t] += from_y[to, h]
-
-            @pl.when(z < to)
-            def _():
-                @pl.when(z > 0)
-                def _():
-                    up_copy(to, h, t).wait_recv()
-                    acc[h, t] += from_low[to, h]
-
-                up_copy(to, h, t).start()
-
-            @pl.when(z > to)
-            def _():
-                @pl.when(z < nz - 1)
-                def _():
-                    down_copy(to, h, t).wait_recv()
-                    acc[h, t] += from_high[to, h]
-
-                down_copy(to, h, t).start()
+        begin(h)
+        loop(nz, lambda i: give(h, 1, i))
+        loop(nz, lambda i: take(h, 1, i))
+        for i, to in enumerate(order):
+            if h:
+                pass_on(h - 1, to)
+            give(h, 0, i)
+        loop(nz, lambda i: take(h, 0, i))
+    for to in order:
+        pass_on(SPLIT - 1, to)
 
     for h in range(SPLIT):
         @pl.when(z > 0)
@@ -275,10 +311,11 @@
         out[h * part : (h + 1) * part, :] = acc[h, me].astype(out.dtype)
 
     for h in range(SPLIT):
-        each(lambda k: out_copy(h, k).wait_send())
-        each(lambda k: back_copy(h, k).wait_send())
+        for q in range(2):
+            each(lambda k: out_copy(h, q, k).wait_send())
+            each(lambda k: back_copy(h, q, k).wait_send())
         for far in (1, 0):
-            loop(lambda i: core_copy(h, i, far).wait_send())
+            loop(nz, lambda i: core_copy(h, i, far).wait_send())
         for to in order:
             t = owner(to, 0, 0)
             y_copy(to, h).wait_send()
@@ -328,7 +365,7 @@
             pltpu.VMEM((SPLIT, 2 * nz, part, width), f32),
             *[pltpu.VMEM((nz, SPLIT, part, width), f32)] * 3,
             dma(()),
-            *[dma((SPLIT, n))] * 4,
+            *[dma((SPLIT, 2, n))] * 4,
             *[dma((SPLIT, 2 * nz))] * 2,
             *[dma((nz, SPLIT))] * 6,
         ],

time: 85.2 us -> 89.3 us (1.048)
  the two profiles are of different devices: /device:TPU:8 before, /device:TPU:0 now
where the time goes in v4:
time: 89.3 us; the launch traced here: 89.2 us
  Pallas kernels  87.6 us (98%)
  local copies, waits for them, and re-layouts  1.57 us (2%)
    pallas_call x1, Pallas kernels, body(): pl.pallas_call(functools.partial(fused, n), out_shape=jax.ShapeDtypeStruc...  87.6 us

profile of v4, /device:TPU:0, one launch (start us, length us, event | category | flops | bytes accessed | tf_op | source)
XLA Modules:
  0.0 89.2 jit_solution(1924762208469068807)
XLA Ops:
  0.0 87.6 %shard_map.37 = bf16[128,512]{1,0:T(8,128)(2,1)} custom-call(bf16[128,1664]{1,0:T(8,128)(2,1)} %act.1, f32[52,52]{1,0:T(8,128)} %small.1, bf16[1664,8192]{1,0:T(8,128)(2,1)} %w_hbm.1), custom_call_target="tpu_custom_call" | custom-call | tf_op jit(solution)/shard_map/pallas_call | solution.py:347
  87.6 1.6 %copy.5 = bf16[128,512]{1,0:T(8,128)(2,1)} copy(bf16[128,512]{1,0:T(8,128)(2,1)} %shard_map.37) | data formatting | bytes 262144

commit v5 on v4

--- a/solution.py
+++ b/solution.py
@@ -91,8 +91,7 @@
         return pl.ds(pl.multiple_of(base + rank // 2 * rows, ROWS), rows)
 
     overlap = wide - shift
-    first = -(-wide // (2 * LANES)) * LANES
-    cuts = ((0, first), (first, wide - first))
+    cuts = ((0, wide),)
 
     def columns_of(rank, q):
         return pl.ds(pl.multiple_of(rank % 2 * shift + cuts[q][0], LANES), cuts[q][1])
@@ -168,7 +167,7 @@
         values = butterfly([pieced[i, at : at + ROWS, :] for i in range(pieces)])
         own[at : at + ROWS, :] = jnp.concatenate(values, axis=1)
     pl.semaphore_wait(barrier, n - 1)
-    stages = [(h, q) for h in range(SPLIT) for q in range(2)]
+    stages = [(h, q) for h in range(SPLIT) for q in range(len(cuts))]
     for h, q in stages:
         each(lambda k: out_copy(h, q, k).start())
         got[h, me, :, pl.ds(*cuts[q])] = own[rows_of(me, h * part), columns_of(me, q)]
@@ -222,14 +221,9 @@
                 back[h, side, :, pl.ds(at, size)].astype(jnp.bfloat16)
             )
 
-    def product(h, q, t):
+    def product(h, t):
         columns = pl.ds(pl.multiple_of(t * width, LANES), width)
-        terms = [
-            dot(rotated[h, :, pl.ds(side * shift + at, size)],
-                w_v[pl.ds(side * shift + at, size), columns])
-            for side, at, size in spans(q)
-        ]
-        return terms[0] + terms[1]
+        return dot(rotated[h], w_v[:, columns])
 
     def loop(count, action):
         def step(i, carry):
@@ -243,20 +237,14 @@
         if h == 0:
             w_copy.wait()
 
-        def tile(t):
-            acc[h, t] = product(h, 0, t)
-
-        loop(n, tile)
-        receive(h, 1)
-
     def give(h, far, i):
         t = owner(place_of(i), far, 1)
-        acc[h, t] += product(h, 1, t)
+        acc[h, t] = product(h, t)
         core_copy(h, i, far).start()
 
     def take(h, far, i):
         t = owner(place_of(i), far, 0)
-        acc[h, t] += product(h, 1, t)
+        acc[h, t] = product(h, t)
         core_copy(h, i, far).wait_recv()
         acc[h, t] += from_core[h, (1 - far) * nz + i]
         if far:
@@ -311,7 +299,7 @@
         out[h * part : (h + 1) * part, :] = acc[h, me].astype(out.dtype)
 
     for h in range(SPLIT):
-        for q in range(2):
+        for q in range(len(cuts)):
             each(lambda k: out_copy(h, q, k).wait_send())
             each(lambda k: back_copy(h, q, k).wait_send())
         for far in (1, 0):
@@ -365,7 +353,7 @@
             pltpu.VMEM((SPLIT, 2 * nz, part, width), f32),
             *[pltpu.VMEM((nz, SPLIT, part, width), f32)] * 3,
             dma(()),
-            *[dma((SPLIT, 2, n))] * 4,
+            *[dma((SPLIT, 1, n))] * 4,
             *[dma((SPLIT, 2 * nz))] * 2,
             *[dma((nz, SPLIT))] * 6,
         ],

time: 89.3 us -> 82.8 us (0.927)
  the two profiles are of different devices: /device:TPU:0 before, /device:TPU:8 now
where the time goes in v5:
time: 82.8 us; the launch traced here: 81.9 us
  Pallas kernels  80.3 us (97%)
  local copies, waits for them, and re-layouts  1.57 us (2%)
    pallas_call x1, Pallas kernels, body(): pl.pallas_call(functools.partial(fused, n), out_shape=jax.ShapeDtypeStruc...  80.3 us

profile of v5, /device:TPU:8, one launch (start us, length us, event | category | flops | bytes accessed | tf_op | source)
XLA Modules:
  0.0 81.9 jit_solution(1417555502703260942)
XLA Ops:
  0.0 80.3 %shard_map.37 = bf16[128,512]{1,0:T(8,128)(2,1)} custom-call(bf16[128,1664]{1,0:T(8,128)(2,1)} %act.1, f32[52,52]{1,0:T(8,128)} %small.1, bf16[1664,8192]{1,0:T(8,128)(2,1)} %w_hbm.1), custom_call_target="tpu_custom_call" | custom-call | tf_op jit(solution)/shard_map/pallas_call | solution.py:335
  80.3 1.6 %copy.5 = bf16[128,512]{1,0:T(8,128)(2,1)} copy(bf16[128,512]{1,0:T(8,128)(2,1)} %shard_map.37) | data formatting | bytes 262144
